TPU v7x, 32 devices: a whole 2x2x4 slice. The times are simulated.
32 devices in a mesh: shot: 4 (over x, core), rcv: 8 (over z, y).
Axes of the slice: x: 2, y: 2, z: 4, core: 2. Of those that a mesh axis runs over, the one named last changes fastest.
Arguments:
- response: bfloat16 [128, 128, 64], P('shot', 'rcv'), may hold values from -0.0625 to 0.0625
- traces: bfloat16 [128, 64, 512], P('shot', 'rcv'), may hold values from -6 to 6
Outputs:
- multiples: bfloat16 [128, 64, 512], P('shot', 'rcv')
All inputs are finite; a program needn't handle non-finite values.
Results may differ from a plain program's by a relative error of at most 0.001.
Values may be sent and summed in bfloat16 or wider, within the bound.
A program may use at most 256 MiB of HBM per device.

v0:
```python
import jax
import jax.numpy as jnp
from jax import lax
from jax.sharding import PartitionSpec as P


def banded(resp_piece):
    shots_here = resp_piece.shape[0]
    rows_in = resp_piece.shape[1]
    tap_count = resp_piece.shape[2]
    reversed_taps = jnp.transpose(resp_piece[:, :, ::-1], (2, 0, 1))
    lead = jnp.zeros((1, shots_here, rows_in), resp_piece.dtype)
    trail = jnp.zeros((tap_count, shots_here, rows_in), resp_piece.dtype)
    pattern = jnp.concatenate([lead, reversed_taps, trail], axis=0)
    repeated = jnp.tile(pattern, (tap_count, 1, 1))[: 2 * tap_count * tap_count]
    return repeated.reshape(tap_count, 2 * tap_count, shots_here, rows_in)


def contract(resp_piece, data_piece):
    shots_here = resp_piece.shape[0]
    tap_count = resp_piece.shape[2]
    rows_in = data_piece.shape[0]
    rcv_here = data_piece.shape[1]
    samples = data_piece.shape[2]
    blocks = samples // tap_count
    band = banded(resp_piece)
    padded = jnp.pad(data_piece, ((0, 0), (0, 0), (tap_count, 0)))
    tiles = padded.reshape(rows_in, rcv_here, blocks + 1, tap_count)
    windows = jnp.concatenate([tiles[:, :, :blocks], tiles[:, :, 1:]], axis=3)
    product = jnp.einsum("uvsk,krbv->srbu", band, windows, preferred_element_type=jnp.float32)
    return product.reshape(shots_here, rcv_here * samples)


def shards(response, traces):
    shots_here = response.shape[0]
    rcv_here = traces.shape[1]
    samples = traces.shape[2]
    responses_all = lax.all_gather(response, "rcv", axis=1, tiled=True)
    running = contract(responses_all, lax.all_gather(traces, "shot", axis=0, tiled=True))
    return running.reshape(shots_here, rcv_here, samples).astype(jnp.bfloat16)


def solution(mesh):
    placed = (P("shot", "rcv", None), P("shot", "rcv", None))
    return jax.shard_map(
        shards, mesh=mesh, in_specs=placed, out_specs=P("shot", "rcv", None), check_vma=False
    )
```

profile of v0, /device:TPU:0, one launch (start us, length us, event | category | flops | bytes accessed | tf_op | source)
XLA Modules:
  0.0 322.5 jit_solution(11808536504618366029)
XLA Ops:
  6.5 0.0 all-gather.2.cloned.1.call-start
  6.5 0.7 all-gather.2.cloned.1.call-update
  7.3 34.9 %all_gather.7 = bf16[32,128,64]{2,1,0:T(8,128)(2,1)S(1)} all-gather(bf16[32,16,64]{2,1,0:T(8,128)(2,1)} %param.2), channel_id=1, replica_groups=mesh['shot'=4,'rcv'=8] {'rcv'}, dimensions={1}, use_global_device_ids=true | all-gather | bytes 589824 | tf_op jit(solution)/shard_map/all_gather | solution.py:38
  42.1 2.9 rev.3
  45.0 0.1 pad.7.clone
  45.1 0.9 maximum_maximum_fusion
  46.0 1.3 copy.14
  47.3 28.0 %tile.4 = bf16[64,129,32,128]{3,2,1,0:T(8,128)(2,1)} broadcast(bf16[129,32,128]{2,1,0:T(8,128)(2,1)S(1)} %copy.14), dimensions={1,2,3} | broadcast | bytes 68689920 | tf_op jit(solution)/shard_map/tile | solution.py:15
  75.3 44.3 %slice.14 = bf16[8192,32,128]{2,1,0:T(8,128)(2,1)} slice(bf16[8256,32,128]{2,1,0:T(8,128)(2,1)} %bitcast.4), slice={[0:8192], [0:32], [0:128]} | slice | bytes 134217728 | tf_op jit(solution)/shard_map/slice | solution.py:15
  119.6 150.2 %copy.19 = bf16[64,128,32,128]{1,0,3,2:T(8,128)(2,1)} copy(bf16[64,128,32,128]{3,2,1,0:T(8,128)(2,1)} %bitcast.5) | data formatting | bytes 134217728 | tf_op jit(solution)/shard_map/reshape | solution.py:16
  269.8 0.0 all-gather.2.cloned.1.call-done
  269.8 1.9 copy.11
  271.7 0.1 pad.4
  271.8 0.5 fusion.14
  272.3 2.0 copy.21
  274.4 0.0 copy-start
  274.4 2.1 copy.20
  276.4 0.0 copy-done
  276.4 38.1 %fusion.10 = bf16[32,8,8,64]{3,2,0,1:T(8,128)(2,1)S(1)} fusion(bf16[64,128,32,128]{1,0,3,2:T(8,128)(2,1)} %copy.19, bf16[128,8,8,64]{3,2,0,1:T(8,128)(2,1)S(1)} %copy-done, bf16[128,8,8,64]{3,2,0,1:T(8,128)(2,1)} %copy.20), kind=kOutput, calls=%fused_computation.8 | convolution fusion | flops 4299292672 | bytes 69468160 | tf_op jit(solution)/shard_map/uvsk,krbv->srbu/dot_general | solution.py:30
  314.5 0.3 convert_element_type.13
  314.8 0.9 copy.16
  (2 shorter events, 0.0 us)
Async XLA Ops:
  6.5 263.3 %all-gather.2.cloned.1.call-start = ((), (), s32[]{:S(2)}) async-start(), calls=%async_computation | async-start | bytes 1310720 | tf_op jit(solution)/shard_map/all_gather | solution.py:39
  274.4 2.1 copy-start
Sparse Core Ops, SparseCore 0:
  8.9 19.4 all-gather.1
where the time goes:
time: 324 us; the launch traced here: 323 us
  local copies, waits for them, and re-layouts  235 us (73%)
  matrix products  38.1 us (12%)
  blocking collectives  34.9 us (11%)
  between operations  13.5 us (4%)
    reshape x1, local copies, waits for them, and re-layouts, banded(): return repeated.reshape(tap_count, 2 * tap_count, shots_here, rows_in)  150 us
    slice x1, local copies, waits for them, and re-layouts, banded(): repeated = jnp.tile(pattern, (tap_count, 1, 1))[:2 * tap_count * tap_count]  44.3 us
    dot_general x1, matrix products, contract(): jnp.einsum('uvsk,krbv->srbu', band, windows, preferred_element_type=jnp.f...  38.1 us
    all_gather x1, blocking collectives, shards(): responses_all = lax.all_gather(response, 'rcv', axis=1, tiled=True)  34.9 us
    another operation x1, local copies, waits for them, and re-layouts, banded(): repeated = jnp.tile(pattern, (tap_count, 1, 1))[:2 * tap_count * tap_count]  28 us
  transfers between devices with their start and end apart: 1, of which 0 were waited for; matrix products, arithmetic and copies ran while one was open for 71% of the time, Pallas kernels for 0%

commit v1 on v0

--- a/solution.py
+++ b/solution.py
@@ -35,7 +35,9 @@
     shots_here = response.shape[0]
     rcv_here = traces.shape[1]
     samples = traces.shape[2]
-    responses_all = lax.all_gather(response, "rcv", axis=1, tiled=True)
+    responses_all = jnp.concatenate(
+        lax.all_to_all(jnp.stack([response] * lax.axis_size("rcv")), "rcv", 0, 0), axis=1
+    )
     running = contract(responses_all, lax.all_gather(traces, "shot", axis=0, tiled=True))
     return running.reshape(shots_here, rcv_here, samples).astype(jnp.bfloat16)
 

time: 324 us -> 314 us (0.969)
  blocking collectives: 34.9 us -> 0 us
  waiting for transfers between devices: 0.71 us -> 15.1 us
  starting transfers between devices: 0.01 us -> 7.31 us
    all_gather x1 -> x0, blocking collectives: 34.9 us -> none  [shards(): responses_all = lax.all_gather(response, 'rcv', axis=1, tiled=True)]
    all_to_all x0 -> x1, waiting for transfers between devices: none -> 14.4 us  [shards(): lax.all_to_all(jnp.stack([response] * lax.axis_size('rcv')), 'rcv', 0, 0)]
    all_to_all x0 -> x1, starting transfers between devices: none -> 7.31 us  [shards(): lax.all_to_all(jnp.stack([response] * lax.axis_size('rcv')), 'rcv', 0, 0)]
  transfers between devices with their start and end apart: 1 -> 2, of which waited for: 0 -> 1; matrix products, arithmetic and copies ran while one was open for 71% -> 74% of each run, Pallas kernels for 0% -> 0%
where the time goes in v1:
time: 314 us; the launch traced here: 313 us
  local copies, waits for them, and re-layouts  238 us (76%)
  matrix products  38.1 us (12%)
  waiting for transfers between devices  15.1 us (5%)
  between operations  13.5 us (4%)
  starting transfers between devices  7.31 us (2%)
    reshape x1, local copies, waits for them, and re-layouts, banded(): return repeated.reshape(tap_count, 2 * tap_count, shots_here, rows_in)  150 us
    slice x1, local copies, waits for them, and re-layouts, banded(): repeated = jnp.tile(pattern, (tap_count, 1, 1))[:2 * tap_count * tap_count]  44.3 us
    dot_general x1, matrix products, contract(): jnp.einsum('uvsk,krbv->srbu', band, windows, preferred_element_type=jnp.f...  38.1 us
    another operation x1, local copies, waits for them, and re-layouts, banded(): repeated = jnp.tile(pattern, (tap_count, 1, 1))[:2 * tap_count * tap_count]  28 us
    all_to_all x1, waiting for transfers between devices, shards(): lax.all_to_all(jnp.stack([response] * lax.axis_size('rcv')), 'rcv', 0, 0)  14.4 us
    all_to_all x1, starting transfers between devices, shards(): lax.all_to_all(jnp.stack([response] * lax.axis_size('rcv')), 'rcv', 0, 0)  7.31 us
  transfers between devices with their start and end apart: 2, of which 1 were waited for; matrix products, arithmetic and copies ran while one was open for 74% of the time, Pallas kernels for 0%

profile of v1, /device:TPU:0, one launch (start us, length us, event | category | flops | bytes accessed | tf_op | source)
XLA Modules:
  0.0 312.9 jit_solution(14104999835247984064)
XLA Ops:
  6.5 0.0 all-gather.2.cloned.1.call-start
  6.5 0.7 all-gather.2.cloned.1.call-update
  7.3 1.0 stack.2
  8.3 1.5 reshape.27
  9.8 7.3 %all-to-all-start = ((bf16[8,2,16384]{2,1,0:T(2,128)(2,1)}), bf16[8,2,16384]{2,1,0:T(2,128)(2,1)S(1)}, u32[]{:S(2)}, u32[]{:S(2)}) async-start(bf16[8,2,16384]{2,1,0:T(2,128)(2,1)} %reshape.27), calls=%async_computation | async-start | bytes 1048576 | tf_op jit(solution)/shard_map/all_to_all | solution.py:39
  17.1 0.1 pad.7.clone
  17.2 14.4 %all-to-all-done = bf16[8,2,16384]{2,1,0:T(2,128)(2,1)S(1)} async-done(((bf16[8,2,16384]{2,1,0:T(2,128)(2,1)}), bf16[8,2,16384]{2,1,0:T(2,128)(2,1)S(1)}, u32[]{:S(2)}, u32[]{:S(2)}) %all-to-all-start) | async-done | bytes 524320 | tf_op jit(solution)/shard_map/all_to_all | solution.py:39
  31.6 0.7 reshape.28
  32.3 0.3 copy.20
  32.6 2.9 rev.3
  35.5 0.9 maximum_maximum_fusion
  36.3 1.3 copy.21
  37.7 28.0 %tile.4 = bf16[64,129,32,128]{3,2,1,0:T(8,128)(2,1)} broadcast(bf16[129,32,128]{2,1,0:T(8,128)(2,1)S(1)} %copy.21), dimensions={1,2,3} | broadcast | bytes 68689920 | tf_op jit(solution)/shard_map/tile | solution.py:15
  65.6 44.3 %slice.14 = bf16[8192,32,128]{2,1,0:T(8,128)(2,1)} slice(bf16[8256,32,128]{2,1,0:T(8,128)(2,1)} %bitcast.6), slice={[0:8192], [0:32], [0:128]} | slice | bytes 134217728 | tf_op jit(solution)/shard_map/slice | solution.py:15
  109.9 150.2 %copy.26 = bf16[64,128,32,128]{1,0,3,2:T(8,128)(2,1)} copy(bf16[64,128,32,128]{3,2,1,0:T(8,128)(2,1)} %bitcast.7) | data formatting | bytes 134217728 | tf_op jit(solution)/shard_map/reshape | solution.py:16
  260.2 0.0 all-gather.2.cloned.1.call-done
  260.2 1.9 copy.17
  262.1 0.1 pad.4
  262.2 0.5 fusion.14
  262.7 2.0 copy.28
  264.7 0.0 copy-start
  264.7 2.0 copy.27
  266.8 0.0 copy-done
  266.8 38.1 %fusion.10 = bf16[32,8,8,64]{3,2,0,1:T(8,128)(2,1)S(1)} fusion(bf16[64,128,32,128]{1,0,3,2:T(8,128)(2,1)} %copy.26, bf16[128,8,8,64]{3,2,0,1:T(8,128)(2,1)S(1)} %copy-done, bf16[128,8,8,64]{3,2,0,1:T(8,128)(2,1)} %copy.27), kind=kOutput, calls=%fused_computation.8 | convolution fusion | flops 4299292672 | bytes 69468160 | tf_op jit(solution)/shard_map/uvsk,krbv->srbu/dot_general | solution.py:30
  304.9 0.3 convert_element_type.13
  305.2 0.9 copy.23
  (2 shorter events, 0.0 us)
Async XLA Ops:
  6.5 253.6 %all-gather.2.cloned.1.call-start = ((), (), s32[]{:S(2)}) async-start(), calls=%async_computation.1 | async-start | bytes 1310720 | tf_op jit(solution)/shard_map/all_gather | solution.py:41
  9.8 21.8 %all-to-all-start = ((bf16[8,2,16384]{2,1,0:T(2,128)(2,1)}), bf16[8,2,16384]{2,1,0:T(2,128)(2,1)S(1)}, u32[]{:S(2)}, u32[]{:S(2)}) async-start(bf16[8,2,16384]{2,1,0:T(2,128)(2,1)} %reshape.27), calls=%async_computation | async-start | bytes 1048576 | tf_op jit(solution)/shard_map/all_to_all | solution.py:39
  264.7 2.1 copy-start
Sparse Core Ops, SparseCore 0:
  8.9 19.4 all-gather.1
